TPU v7x, 32 devices: a whole 2x2x4 slice. The times are simulated.
32 devices in a mesh: row: 4 (over y, x), col: 8 (over z, core).
Axes of the slice: x: 2, y: 2, z: 4, core: 2. Of those that a mesh axis runs over, the one named last changes fastest.
Arguments:
- features: bfloat16 [16384, 256], P(('col', 'row')), may hold values from -6 to 6
- weight: bfloat16 [256, 256], replicated, may hold values from -0.375 to 0.375
- cotangent: bfloat16 [16384, 256], P(('row', 'col')), may hold values from -6 to 6
- block_index: int32 [4, 8, 32], P('row', 'col'), may hold values from 0 to 511, as said below
- block_count: int32 [4, 8], P('row', 'col'), may hold values from 1 to 32, as said below
- block_values: bfloat16 [4, 8, 32, 128, 128], P('row', 'col'), may hold values from -0.25 to 0.25
Outputs:
- hidden_out: bfloat16 [16384, 256], P(('row', 'col'))
- input_grad: bfloat16 [16384, 256], P(('col', 'row'))
- weight_grad: float32 [256, 256], replicated
Inputs may be any that keep to these rules, and one draw needn't show every extreme that they name: `block_index`: the 32 entries of one tile are distinct; slots at or after the tile's count hold blocks that are not used. `block_count`: at least one tile holds exactly 32 blocks.
All inputs are finite; a program needn't handle non-finite values.
Results may differ from a plain program's by a relative error of at most 0.015.
Values may be sent and summed in bfloat16 or wider, within the bound.
No kernel may reach another device: no remote copies, remote signals or barrier semaphores. Data moves between devices by JAX's collectives and lax.ppermute only.
A program may use at most 64 MiB of HBM per device.

v0:
```python
import math
import jax
import jax.numpy as jnp
from jax import lax
from jax.sharding import PartitionSpec as P

GROUP = 32


def forward_tile(blocks_in, values, index, count, rows_out):
    ncols = blocks_in.shape[0]
    size = blocks_in.shape[1]
    width = blocks_in.shape[2]
    lanes = jnp.arange(GROUP, dtype=jnp.int32)
    targets = jnp.arange(rows_out, dtype=jnp.int32)

    def forward_advance(group_id, totals):
        start = (group_id * GROUP).astype(jnp.int32)
        live = start + lanes < count
        picked = jnp.take(blocks_in, index % ncols, axis=0)
        product = jnp.einsum("gij,gjd->gid", values, picked, preferred_element_type=jnp.float32)
        selector = ((index // ncols)[None, :] == targets[:, None]) & live[None, :]
        return totals + jnp.einsum(
            "rg,gid->rid", selector.astype(jnp.float32), product, precision=lax.Precision.HIGHEST
        )

    zeros = jnp.zeros((rows_out, size, width), jnp.float32)
    groups = (count + GROUP - 1) // GROUP
    return lax.fori_loop(jnp.int32(0), groups, forward_advance, zeros)


def backward_tile(blocks_grad, values, index, count, cols_out):
    size = blocks_grad.shape[1]
    width = blocks_grad.shape[2]
    lanes = jnp.arange(GROUP, dtype=jnp.int32)
    targets = jnp.arange(cols_out, dtype=jnp.int32)

    def backward_advance(group_id, totals):
        start = (group_id * GROUP).astype(jnp.int32)
        live = start + lanes < count
        picked = jnp.take(blocks_grad, index // cols_out, axis=0)
        product = jnp.einsum("gij,gid->gjd", values, picked, preferred_element_type=jnp.float32)
        selector = ((index % cols_out)[None, :] == targets[:, None]) & live[None, :]
        return totals + jnp.einsum(
            "cg,gjd->cjd", selector.astype(jnp.float32), product, precision=lax.Precision.HIGHEST
        )

    zeros = jnp.zeros((cols_out, size, width), jnp.float32)
    groups = (count + GROUP - 1) // GROUP
    return lax.fori_loop(jnp.int32(0), groups, backward_advance, zeros)


def body(features, weight, cotangent, block_index, block_count, block_values):
    row_total = lax.axis_size("row")
    col_total = lax.axis_size("col")
    rows = features.shape[0]
    width = features.shape[1]
    size = block_values.shape[-1]
    block_rows = rows * col_total // size
    block_cols = rows * row_total // size
    index = block_index[0, 0]
    count = block_count[0, 0]
    values = block_values[0, 0]
    gathered = lax.all_gather(features, "row", axis=0, tiled=True)
    projected = jnp.dot(gathered, weight, preferred_element_type=jnp.float32).astype(jnp.bfloat16)
    partial_out = forward_tile(
        projected.reshape(block_cols, size, width), values, index, count, block_rows
    )
    summed_out = lax.psum_scatter(
        partial_out.reshape(block_rows * size, width).astype(jnp.bfloat16),
        "col",
        scatter_dimension=0,
        tiled=True,
    )
    grad_rows = lax.all_gather(cotangent, "col", axis=0, tiled=True)
    partial_back = backward_tile(
        grad_rows.reshape(block_rows, size, width), values, index, count, block_cols
    )
    partial_back = partial_back.reshape(block_cols * size, width)
    grad_sum = lax.psum_scatter(
        partial_back.astype(jnp.bfloat16), "row", scatter_dimension=0, tiled=True
    ).astype(jnp.float32)
    input_grad = jnp.dot(
        grad_sum, weight.astype(jnp.float32).T, precision=lax.Precision.HIGHEST
    ).astype(jnp.bfloat16)
    term = jnp.einsum(
        "nd,ne->de", gathered, partial_back.astype(jnp.bfloat16), preferred_element_type=jnp.float32
    )
    total = lax.psum(term, ("row", "col"))
    nodes = rows * row_total * col_total
    weight_grad = total / math.sqrt(nodes)
    return (summed_out, input_grad, weight_grad)


def solution(mesh):
    in_specs = (
        P(("col", "row"), None),
        P(),
        P(("row", "col"), None),
        P("row", "col", None),
        P("row", "col"),
        P("row", "col", None, None, None),
    )
    out_specs = (P(("row", "col"), None), P(("col", "row"), None), P())
    return jax.shard_map(body, mesh=mesh, in_specs=in_specs, out_specs=out_specs, check_vma=False)
```

profile of v0, /device:TPU:0, one launch (start us, length us, event | category | flops | bytes accessed | tf_op | source)
XLA Modules:
  0.0 277.0 jit_solution(4447913578105518089)
XLA Ops:
  8.0 0.7 all-gather.3.cloned.1.call-update
  11.4 30.1 %all-gather.5.cloned.1.call-done = bf16[4096,256]{1,0:T(8,128)(2,1)} async-done(((bf16[512,256]{1,0:T(8,128)(2,1)}), bf16[4096,256]{1,0:T(8,128)(2,1)}) %all-gather.5.cloned.1.call-update) | async-done | bytes 2097168 | tf_op jit(solution)/shard_map/all_gather | solution.py:75
  41.5 3.6 %gather_fusion.1 = bf16[32,128,256]{2,1,0:T(8,128)(2,1)} fusion(bf16[32,128,256]{2,1,0:T(8,128)(2,1)} %bitcast.94, s32[1024]{0:T(1024)S(1)} %pad_clamp_fusion.1), kind=kCustom, calls=%fused_computation.1 | custom fusion | bytes 4194432 | tf_op jit(solution)/shard_map/while/body/jit(_take)/gather | solution.py:41
  45.8 15.6 %while.34 = (s32[]{:T(128)}, f32[16,128,256]{2,0,1:T(8,128)S(1)}, s32[]{:T(128)}, s32[32]{0:T(128)S(1)}, s32[32]{0:T(128)S(1)}, /*index=5*/s32[]{:T(128)}, s32[3...) while((s32[]{:T(128)}, f32[16,128,256]{2,0,1:T(8,128)S(1)}, ...), condition=%wide.region_4.5_spmd.clone, body=%wide.region_3.4_spmd.clone.sunk | while | flops 471336928 | bytes 24118400 | solution.py:50
  46.5 4.6 %fusion.69 = f32[32,256,128]{2,1,0:T(8,128)} fusion(bf16[32,128,128]{2,1,0:T(8,128)(2,1)} %get-tuple-element.889, bf16[32,128,256]{2,1,0:T(8,128)(2,1)} %get-tuple-element.888, pred[32]{0:T(512)(128)(4,1)S(1)} %get-tuple-element.805), kind=kOutput, calls=%fused_computation.7.clone.1 | convolution fusion | flops 269484032 | bytes 7340064 | tf_op jit(solution)/shard_map/while/body/gij,gid->gjd/dot_general | solution.py:42
  51.1 5.5 %copy.20 = f32[32,256,128]{1,0,2:T(8,128)} copy(f32[32,256,128]{2,1,0:T(8,128)} %fusion.69) | data formatting | bytes 8388608 | tf_op jit(solution)/shard_map/while/body/gij,gid->gjd/dot_general | solution.py:42
  56.6 4.8 %fusion.70 = f32[16,128,256]{2,0,1:T(8,128)S(1)} fusion(f32[16,128,256]{2,0,1:T(8,128)S(1)} %get-tuple-element.871, f32[32,256,128]{1,0,2:T(8,128)} %copy.20, s32[32]{0:T(128)S(1)} %and_select_fusion.6, pred[32]{0:T(512)(128)(4,1)S(1)} %get-tuple-element.806), kind=kOutput, calls=%fused_computation.10.clone.1 | convolution fusion | flops 201851904 | bytes 8388768 | tf_op jit(solution)/shard_map/while/body/cg,gjd->cjd/dot_general | solution.py:44
  61.4 1.1 copy.17
  62.6 6.7 %all-gather.3.cloned.1.call-done = bf16[2048,256]{1,0:T(8,128)(2,1)} async-done(((bf16[512,256]{1,0:T(8,128)(2,1)}), bf16[2048,256]{1,0:T(8,128)(2,1)}) %all-gather.3.cloned.1.call-update) | async-done | bytes 1048592 | tf_op jit(solution)/shard_map/all_gather | solution.py:64
  69.3 2.5 convolution_bitcast_fusion
  72.4 2.5 broadcast_in_dim.62
  74.9 18.6 %while.35 = (s32[]{:T(128)}, f32[32,128,256]{2,0,1:T(8,128)}, s32[]{:T(128)}, s32[1,32]{1,0:T(1,128)S(1)}, s32[32]{0:T(128)S(1)}, /*index=5*/s32[1,32]{1,0:T(1,1...) while((s32[]{:T(128)}, f32[32,128,256]{2,0,1:T(8,128)}, ...), condition=%wide.region_1.2_spmd.clone.clone, body=%wide.region_0.1_spmd.clone.clone.sunk | while | flops 673190272 | bytes 32511760 | solution.py:29
  75.6 0.7 gather_fusion
  76.3 4.0 %fusion.76 = f32[32,256,128]{2,1,0:T(8,128)} fusion(bf16[32,128,128]{2,1,0:T(8,128)(2,1)} %get-tuple-element.856, bf16[32,128,256]{2,1,0:T(8,128)(2,1)S(1)} %gather_fusion, pred[32]{0:T(512)(128)(4,1)S(1)} %get-tuple-element.818), kind=kOutput, calls=%fused_computation.30.clone.1 | convolution fusion | flops 269484032 | bytes 7340064 | tf_op jit(solution)/shard_map/while/body/gij,gjd->gid/dot_general | solution.py:21
  80.3 5.5 %copy.21 = f32[32,256,128]{1,0,2:T(8,128)} copy(f32[32,256,128]{2,1,0:T(8,128)} %fusion.76) | data formatting | bytes 8388608 | tf_op jit(solution)/shard_map/while/body/gij,gjd->gid/dot_general | solution.py:21
  85.8 7.7 %fusion.78 = f32[32,128,256]{2,0,1:T(8,128)} fusion(f32[32,128,256]{2,0,1:T(8,128)} %get-tuple-element.834, f32[32,256,128]{1,0,2:T(8,128)} %copy.21, s32[32]{0:T(128)S(1)} %fusion.77, pred[32]{0:T(512)(128)(4,1)S(1)} %get-tuple-element.819), kind=kOutput, calls=%fused_computation.29.clone.1 | convolution fusion | flops 403703808 | bytes 12583072 | tf_op jit(solution)/shard_map/while/body/rg,gid->rid/dot_general | solution.py:23
  93.5 2.5 convert_element_type.25
  96.0 2.5 copy.11
  98.6 103.3 %all-reduce.2.cloned.1.call-done = f32[256,256]{0,1:T(8,128)} async-done(((f32[256,256]{0,1:T(8,128)}), f32[256,256]{0,1:T(8,128)}) %all-reduce.2.cloned.1.call-update) | async-done | bytes 262160 | tf_op jit(solution)/shard_map/psum | solution.py:89
  201.9 1.0 broadcast_multiply_fusion
  202.9 0.8 copy.13
  203.7 27.9 %reduce-scatter.5.cloned.1.call-done = bf16[512,256]{1,0:T(8,128)(2,1)} async-done(((bf16[2048,256]{1,0:T(8,128)(2,1)}), bf16[512,256]{1,0:T(8,128)(2,1)}) %reduce-scatter.5.cloned.1.call-update) | async-done | bytes 262160 | tf_op jit(solution)/shard_map/reduce_scatter | solution.py:80
  231.7 1.9 convolution_convert_fusion.1
  233.6 36.9 %reduce-scatter.3.cloned.1.call-done = bf16[512,256]{1,0:T(8,128)(2,1)} async-done(((bf16[4096,256]{1,0:T(8,128)(2,1)}), bf16[512,256]{1,0:T(8,128)(2,1)}) %reduce-scatter.3.cloned.1.call-update) | async-done | bytes 262160 | tf_op jit(solution)/shard_map/reduce_scatter | solution.py:69
  (29 shorter events, 5.4 us)
Async XLA Ops:
  7.2 64.7 %copy-start = (bf16[256,256]{1,0:T(8,128)(2,1)S(1)}, bf16[256,256]{1,0:T(8,128)(2,1)}, u32[]{:S(2)}) copy-start(bf16[256,256]{1,0:T(8,128)(2,1)} %param.11) | copy-start | bytes 393220
  7.2 34.3 %all-gather.5.cloned.1.call-start = ((), (), s32[]{:S(2)}) async-start(), calls=%async_computation.4 | async-start | bytes 2359296 | tf_op jit(solution)/shard_map/all_gather | solution.py:75
  7.9 61.3 %all-gather.3.cloned.1.call-start = ((), (), s32[]{:S(2)}) async-start(), calls=%async_computation.2 | async-start | bytes 1310720 | tf_op jit(solution)/shard_map/all_gather | solution.py:64
  8.7 193.3 %all-reduce.2.cloned.1.call-start = ((), (), s32[]{:S(2)}) async-start(), calls=%async_computation.6 | async-start | bytes 524288 | tf_op jit(solution)/shard_map/psum | solution.py:89
  45.1 0.7 copy-start.3
  62.6 9.2 %copy-start.1 = (bf16[16,128,256]{2,1,0:T(8,128)(2,1)}, bf16[16,128,256]{2,1,0:T(8,128)(2,1)S(1)}, u32[]{:S(2)}) copy-start(bf16[16,128,256]{2,1,0:T(8,128)(2,1)S(1)} %copy.17) | copy-start | bytes 3145732
  69.3 2.6 copy-start.2
  71.8 159.9 %reduce-scatter.5.cloned.1.call-start = ((), (), s32[]{:S(2)}) async-start(), calls=%async_computation.5 | async-start | bytes 1310720 | tf_op jit(solution)/shard_map/reduce_scatter | solution.py:80
  72.4 198.1 %reduce-scatter.3.cloned.1.call-start = ((), (), s32[]{:S(2)}) async-start(), calls=%async_computation.3 | async-start | bytes 2359296 | tf_op jit(solution)/shard_map/reduce_scatter | solution.py:69
Sparse Core Ops, SparseCore 0:
  9.6 31.8 all-gather.4
  43.3 25.8 all-gather.2
  75.3 126.5 all-reduce.1
  204.7 26.9 reduce-scatter.4
  234.4 36.0 reduce-scatter.2
where the time goes:
time: 278 us; the launch traced here: 277 us
  waiting for transfers between devices  206 us (74%)
  matrix products  26 us (9%)
  local copies, waits for them, and re-layouts  22.9 us (8%)
  between operations  14.5 us (5%)
  other arithmetic  6.83 us (2%)
    psum x1, waiting for transfers between devices, body(): total = lax.psum(term, ('row', 'col'))  103 us
    reduce_scatter x1, waiting for transfers between devices, body(): lax.psum_scatter(partial_out.reshape(block_rows * size, width).astype(jnp...  36.9 us
    all_gather x1, waiting for transfers between devices, body(): grad_rows = lax.all_gather(cotangent, 'col', axis=0, tiled=True)  30.1 us
    reduce_scatter x1, waiting for transfers between devices, body(): lax.psum_scatter(partial_back.astype(jnp.bfloat16), 'row', scatter_dimens...  27.9 us
    dot_general x1, matrix products, forward_advance(): jnp.einsum('rg,gid->rid', selector.astype(jnp.float32), product, precisio...  7.68 us
    all_gather x1, waiting for transfers between devices, body(): gathered = lax.all_gather(features, 'row', axis=0, tiled=True)  6.68 us
  transfers between devices with their start and end apart: 5, of which 5 were waited for; matrix products, arithmetic and copies ran while one was open for 19% of the time, Pallas kernels for 0%

commit v1 on v0

--- a/solution.py
+++ b/solution.py
@@ -86,7 +86,8 @@
     term = jnp.einsum(
         "nd,ne->de", gathered, partial_back.astype(jnp.bfloat16), preferred_element_type=jnp.float32
     )
-    total = lax.psum(term, ("row", "col"))
+    parts = lax.all_gather(term, ("row", "col"), axis=0, tiled=False)
+    total = parts.sum(axis=0)
     nodes = rows * row_total * col_total
     weight_grad = total / math.sqrt(nodes)
     return (summed_out, input_grad, weight_grad)

time: 278 us -> 232 us (0.83)
  waiting for transfers between devices: 206 us -> 150 us
  local copies, waits for them, and re-layouts: 22.9 us -> 32.4 us
    psum x1 -> x0, waiting for transfers between devices: 103 us -> none  [body(): total = lax.psum(term, ('row', 'col'))]
    all_gather x0 -> x1, waiting for transfers between devices: none -> 85.5 us  [body(): parts = lax.all_gather(term, ('row', 'col'), axis=0, tiled=False)]
    reduce_scatter x1, waiting for transfers between devices: 27.9 us -> 1.26 us  [body(): lax.psum_scatter(partial_back.astype(jnp.bfloat16), 'row', scatter_dimens...]
    unnamed x9, local copies, waits for them, and re-layouts: 1.25 us -> 11 us
    reduce_scatter x1, waiting for transfers between devices: 36.9 us -> 27.3 us  [body(): lax.psum_scatter(partial_out.reshape(block_rows * size, width).astype(jnp...]
  transfers between devices with their start and end apart: 5 -> 5, of which waited for: 5 -> 5; matrix products, arithmetic and copies ran while one was open for 19% -> 28% of each run, Pallas kernels for 0% -> 0%
where the time goes in v1:
time: 232 us; the launch traced here: 231 us
  waiting for transfers between devices  150 us (65%)
  local copies, waits for them, and re-layouts  32.4 us (14%)
  matrix products  26.4 us (11%)
  between operations  14.5 us (6%)
  other arithmetic  7.2 us (3%)
    all_gather x1, waiting for transfers between devices, body(): parts = lax.all_gather(term, ('row', 'col'), axis=0, tiled=False)  85.5 us
    all_gather x1, waiting for transfers between devices, body(): grad_rows = lax.all_gather(cotangent, 'col', axis=0, tiled=True)  30.8 us
    reduce_scatter x1, waiting for transfers between devices, body(): lax.psum_scatter(partial_out.reshape(block_rows * size, width).astype(jnp...  27.3 us
    unnamed x9, local copies, waits for them, and re-layouts  11 us
    dot_general x1, matrix products, forward_advance(): jnp.einsum('rg,gid->rid', selector.astype(jnp.float32), product, precisio...  7.76 us
    dot_general x1, local copies, waits for them, and re-layouts, forward_advance(): jnp.einsum('gij,gjd->gid', values, picked, preferred_element_type=jnp.flo...  5.51 us
    dot_general x1, local copies, waits for them, and re-layouts, backward_advance(): jnp.einsum('gij,gid->gjd', values, picked, preferred_element_type=jnp.flo...  5.51 us
    dot_general x1, matrix products, backward_advance(): jnp.einsum('cg,gjd->cjd', selector.astype(jnp.float32), product, precisio...  4.83 us
  transfers between devices with their start and end apart: 5, of which 5 were waited for; matrix products, arithmetic and copies ran while one was open for 28% of the time, Pallas kernels for 0%

profile of v1, /device:TPU:0, one launch (start us, length us, event | category | flops | bytes accessed | tf_op | source)
XLA Modules:
  0.0 231.0 jit_solution(13673392330667548795)
XLA Ops:
  10.7 30.8 %all-gather.7.cloned.1.call-done = bf16[4096,256]{1,0:T(8,128)(2,1)} async-done(((bf16[512,256]{1,0:T(8,128)(2,1)}), bf16[4096,256]{1,0:T(8,128)(2,1)}) %all-gather.7.cloned.1.call-update) | async-done | bytes 2097168 | tf_op jit(solution)/shard_map/all_gather | solution.py:75
  41.5 2.3 gather_fusion.1
  43.8 3.0 %copy.22 = bf16[32,128,256]{1,2,0:T(8,128)(2,1)} copy(bf16[32,128,256]{2,1,0:T(8,128)(2,1)S(1)} %gather_fusion.1) | data formatting | bytes 4194304
  47.4 15.7 %while.34 = (s32[]{:T(128)}, f32[16,128,256]{2,0,1:T(8,128)S(1)}, s32[]{:T(128)}, s32[32]{0:T(128)S(1)}, s32[32]{0:T(128)S(1)}, /*index=5*/s32[]{:T(128)}, s32[3...) while((s32[]{:T(128)}, f32[16,128,256]{2,0,1:T(8,128)S(1)}, ...), condition=%wide.region_4.5_spmd.clone, body=%wide.region_3.4_spmd.clone.sunk | while | flops 471336928 | bytes 24118408 | solution.py:50
  48.1 4.7 %convolution_bitcast_fusion.5 = f32[32,128,256]{1,2,0:T(8,128)} fusion(bf16[32,128,128]{2,1,0:T(8,128)(2,1)} %get-tuple-element.898, bf16[32,128,256]{1,2,0:T(8,128)(2,1)} %get-tuple-element.897, pred[32]{0:T(512)(128)(4,1)S(1)} %get-tuple-element.814), kind=kOutput, calls=%fused_computation.5.clone.1 | convolution fusion | flops 269484032 | bytes 7340064 | tf_op jit(solution)/shard_map/while/body/gij,gid->gjd/dot_general | solution.py:42
  52.7 5.5 %copy.31 = f32[32,128,256]{2,0,1:T(8,128)} copy(f32[32,128,256]{1,2,0:T(8,128)} %convolution_bitcast_fusion.5) | data formatting | bytes 8388608 | tf_op jit(solution)/shard_map/while/body/gij,gid->gjd/dot_general | solution.py:42
  58.3 4.8 %convolution_add_fusion.4 = f32[16,128,256]{2,0,1:T(8,128)S(1)} fusion(f32[16,128,256]{2,0,1:T(8,128)S(1)} %get-tuple-element.880, f32[32,128,256]{2,0,1:T(8,128)} %copy.31, s32[32]{0:T(128)S(1)} %and_select_fusion.6, pred[32]{0:T(512)(128)(4,1)S(1)} %get-tuple-element.815), kind=kOutput, calls=%fused_computation.8.clone.1 | convolution fusion | flops 201851904 | bytes 8388768 | tf_op jit(solution)/shard_map/while/body/cg,gjd->cjd/dot_general | solution.py:44
  63.1 2.1 copy.28
  65.3 4.0 %all-gather.5.cloned.1.call-done = bf16[2048,256]{1,0:T(8,128)(2,1)} async-done(((bf16[512,256]{1,0:T(8,128)(2,1)}), bf16[2048,256]{1,0:T(8,128)(2,1)}) %all-gather.5.cloned.1.call-update) | async-done | bytes 1048592 | tf_op jit(solution)/shard_map/all_gather | solution.py:64
  69.3 2.8 %convolution_bitcast_fusion.2 = f32[256,256]{0,1:T(8,128)} fusion(bf16[2048,256]{1,0:T(8,128)(2,1)} %bitcast.97, bf16[2048,256]{1,0:T(8,128)(2,1)} %all-gather.5.cloned.1.call-done), kind=kOutput, calls=%fused_computation.60 | convolution fusion | flops 268435456 | bytes 2359296 | tf_op jit(solution)/shard_map/nd,ne->de/dot_general | solution.py:86
  72.6 2.5 %broadcast_in_dim.62 = f32[32,128,256]{2,0,1:T(8,128)} broadcast(f32[]{:T(128)} %constant.236.clone.1), dimensions={} | broadcast | bytes 4194308 | tf_op jit(solution)/shard_map/broadcast_in_dim | solution.py:27
  75.1 18.6 %while.35 = (s32[]{:T(128)}, f32[32,128,256]{2,0,1:T(8,128)}, s32[]{:T(128)}, s32[1,32]{1,0:T(1,128)S(1)}, s32[32]{0:T(128)S(1)}, /*index=5*/s32[1,32]{1,0:T(1,1...) while((s32[]{:T(128)}, f32[32,128,256]{2,0,1:T(8,128)}, ...), condition=%wide.region_1.2_spmd.clone.clone, body=%wide.region_0.1_spmd.clone.clone.sunk | while | flops 673190272 | bytes 32511768 | solution.py:29
  76.5 4.0 %convolution_bitcast_fusion.6 = f32[32,128,256]{1,2,0:T(8,128)} fusion(bf16[32,128,128]{2,1,0:T(8,128)(2,1)} %get-tuple-element.865, bf16[32,128,256]{2,1,0:T(8,128)(2,1)S(1)} %gather_fusion, pred[32]{0:T(512)(128)(4,1)S(1)} %get-tuple-element.827), kind=kOutput, calls=%fused_computation.25.clone.1 | convolution fusion | flops 269484032 | bytes 7340064 | tf_op jit(solution)/shard_map/while/body/gij,gjd->gid/dot_general | solution.py:21
  80.5 5.5 %copy.32 = f32[32,128,256]{2,0,1:T(8,128)} copy(f32[32,128,256]{1,2,0:T(8,128)} %convolution_bitcast_fusion.6) | data formatting | bytes 8388608 | tf_op jit(solution)/shard_map/while/body/gij,gjd->gid/dot_general | solution.py:21
  86.0 7.8 %convolution_add_fusion.5 = f32[32,128,256]{2,0,1:T(8,128)} fusion(f32[32,128,256]{2,0,1:T(8,128)} %get-tuple-element.843, f32[32,128,256]{2,0,1:T(8,128)} %copy.32, s32[32]{0:T(128)S(1)} %fusion.60, pred[32]{0:T(512)(128)(4,1)S(1)} %get-tuple-element.828), kind=kOutput, calls=%fused_computation.26.clone.1 | convolution fusion | flops 403703808 | bytes 12583072 | tf_op jit(solution)/shard_map/while/body/rg,gid->rid/dot_general | solution.py:23
  93.8 2.5 %convert_element_type.25 = bf16[32,128,256]{2,0,1:T(8,128)(2,1)S(1)} convert(f32[32,128,256]{2,0,1:T(8,128)} %get-tuple-element.554) | non-fusion elementwise | flops 1048576 | bytes 6291456 | tf_op jit(solution)/shard_map/convert_element_type | solution.py:70
  96.3 2.5 %copy.21 = bf16[32,128,256]{2,1,0:T(8,128)(2,1)} copy(bf16[32,128,256]{2,0,1:T(8,128)(2,1)S(1)} %convert_element_type.25) | data formatting | bytes 4194304 | tf_op jit(solution)/shard_map/convert_element_type | solution.py:70
  98.9 1.3 reduce-scatter.5.cloned.1.call-done
  100.1 1.9 convolution_convert_fusion.1
  102.0 85.5 %all-gather.9.cloned.1.call-done = f32[8192,256]{0,1:T(8,128)} async-done(((f32[256,256]{0,1:T(8,128)}), f32[8192,256]{0,1:T(8,128)}) %all-gather.9.cloned.1.call-update) | async-done | bytes 8388624 | tf_op jit(solution)/shard_map/all_gather | solution.py:89
  187.5 6.8 %copy.26 = f32[32,8,32,256]{3,2,1,0:T(8,128)S(1)} copy(f32[32,8,32,256]{3,1,2,0:T(8,128)} %bitcast.98) | data formatting | bytes 16777216
  194.4 1.9 bitcast_reduce_fusion
  196.4 0.8 copy.24
  197.2 27.3 %reduce-scatter.3.cloned.1.call-done = bf16[512,256]{1,0:T(8,128)(2,1)} async-done(((bf16[4096,256]{1,0:T(8,128)(2,1)}), bf16[512,256]{1,0:T(8,128)(2,1)}) %reduce-scatter.3.cloned.1.call-update) | async-done | bytes 262160 | tf_op jit(solution)/shard_map/reduce_scatter | solution.py:69
  (30 shorter events, 6.1 us)
Async XLA Ops:
  7.2 65.0 %copy-start = (bf16[256,256]{1,0:T(8,128)(2,1)S(1)}, bf16[256,256]{1,0:T(8,128)(2,1)}, u32[]{:S(2)}) copy-start(bf16[256,256]{1,0:T(8,128)(2,1)} %param.11) | copy-start | bytes 393220
  7.2 34.3 %all-gather.7.cloned.1.call-start = ((), (), s32[]{:S(2)}) async-start(), calls=%async_computation.4 | async-start | bytes 2359296 | tf_op jit(solution)/shard_map/all_gather | solution.py:75
  7.9 61.4 %all-gather.5.cloned.1.call-start = ((), (), s32[]{:S(2)}) async-start(), calls=%async_computation.2 | async-start | bytes 1310720 | tf_op jit(solution)/shard_map/all_gather | solution.py:64
  8.7 91.5 %reduce-scatter.5.cloned.1.call-start = ((), (), s32[]{:S(2)}) async-start(), calls=%async_computation.5 | async-start | bytes 1310720 | tf_op jit(solution)/shard_map/reduce_scatter | solution.py:80
  46.7 0.7 copy-start.2
  65.2 122.3 %all-gather.9.cloned.1.call-start = ((), (), s32[]{:S(2)}) async-start(), calls=%async_computation.6 | async-start | bytes 8650752 | tf_op jit(solution)/shard_map/all_gather | solution.py:89
  69.3 2.9 %copy-start.1 = (bf16[2048,256]{1,0:T(8,128)(2,1)S(1)}, bf16[2048,256]{1,0:T(8,128)(2,1)}, u32[]{:S(2)}) copy-start(bf16[2048,256]{1,0:T(8,128)(2,1)} %all-gather.5.cloned.1.call-done) | copy-start | bytes 3145732
  72.1 152.4 %reduce-scatter.3.cloned.1.call-start = ((), (), s32[]{:S(2)}) async-start(), calls=%async_computation.3 | async-start | bytes 2359296 | tf_op jit(solution)/shard_map/reduce_scatter | solution.py:69
Sparse Core Ops, SparseCore 0:
  9.6 31.8 all-gather.6
  43.3 25.8 all-gather.4
  72.2 27.9 reduce-scatter.4
  103.5 84.0 all-gather.8
  190.2 34.2 reduce-scatter.2
